TPU v7x, 128 devices: a whole 4x4x4 slice. The times are simulated.
128 devices in a mesh: dp: 8 (over x_lo, y), expert: 16 (over x_hi, z, core).
Axes of the slice: x: 4 (x_hi: 2, x_lo: 2; x = x_hi * 2 + x_lo), y: 4, z: 4, core: 2. Of those that a mesh axis runs over, the one named last changes fastest.
Arguments:
- tokens: bfloat16 [65536, 2048], P(('dp', 'expert')), may hold values from -6 to 6
- probe: bfloat16 [65536, 2048], P(('dp', 'expert')), may hold values from -20 to 20
- domain: int32 [65536], P(('dp', 'expert')), may hold values from 0 to 21
- mix: float32 [22], replicated, may hold values from 0.5 to 2
- router: bfloat16 [2048, 32], replicated, may hold values from -0.125 to 0.125
- picks: int32 [128, 32, 40], P(('dp', 'expert')), may hold values from 0 to 511, as said below
- w_gate: bfloat16 [2048, 32, 768], P(None, 'expert'), may hold values from -0.125 to 0.125
- w_up: bfloat16 [2048, 32, 768], P(None, 'expert'), may hold values from -0.125 to 0.125
- w_down: bfloat16 [2048, 32, 768], P(None, 'expert'), may hold values from -0.21875 to 0.21875
Outputs:
- domain_loss: float32 [22], replicated
- router_grad: float32 [2048, 32], replicated
- grad_gate: bfloat16 [2048, 32, 768], P('dp', 'expert')
- grad_up: bfloat16 [2048, 32, 768], P('dp', 'expert')
- grad_down: bfloat16 [2048, 32, 768], P('dp', 'expert')
Inputs may be any that keep to these rules, and one draw needn't show every extreme that they name: The 40 picks of one expert on one device are distinct token positions of that device.
All inputs are finite; a program needn't handle non-finite values.
Results may differ from a plain program's by a relative error of at most 0.018.
Values may be sent and summed in bfloat16 or wider, within the bound.
A program may use at most 192 MiB of HBM per device.

v0:
```python
import math
import jax
import jax.numpy as jnp
from jax import lax
from jax.sharding import PartitionSpec as P

BF = jnp.bfloat16
F32 = jnp.float32


def body(tokens, probe, domain, mix, router, picks, w_gate, w_up, w_down):
    token_count, model_width = tokens.shape
    expert_count = router.shape[1]
    slot_count = picks.shape[2]
    pick_count = expert_count * slot_count
    domain_count = mix.shape[0]
    device_count = lax.axis_size("dp") * lax.axis_size("expert")
    flat = picks[0].reshape(pick_count)
    token_ids = jnp.arange(token_count, dtype=jnp.int32)
    select = (flat[:, None] == token_ids[None, :]).astype(BF)
    expert_of = jnp.repeat(jnp.arange(expert_count, dtype=jnp.int32), slot_count)
    own_expert = expert_of[:, None] == jnp.arange(expert_count, dtype=jnp.int32)[None, :]
    outgoing = jnp.dot(select, tokens, preferred_element_type=F32).astype(BF)
    received = lax.all_to_all(
        outgoing.reshape(expert_count, 1, slot_count, model_width),
        "expert",
        split_axis=0,
        concat_axis=1,
        tiled=True,
    )
    logits = jnp.dot(outgoing, router, preferred_element_type=F32)
    gate = jax.nn.sigmoid(jnp.sum(jnp.where(own_expert, logits, 0.0), axis=1))
    pre_gate = jnp.einsum("jsrd,djf->jsrf", received, w_gate, preferred_element_type=F32)
    pre_up = jnp.einsum("jsrd,djf->jsrf", received, w_up, preferred_element_type=F32)
    hidden = (jax.nn.silu(pre_gate) * pre_up).astype(BF)
    result = jnp.einsum("jsrf,djf->jsrd", hidden, w_down, preferred_element_type=F32).astype(BF)
    returned = lax.all_to_all(result, "expert", split_axis=1, concat_axis=0, tiled=True)
    returned = returned.reshape(pick_count, model_width)
    weighted = jnp.where(
        flat[None, :] == token_ids[:, None], gate.astype(BF)[None, :], jnp.zeros((), BF)
    )
    added = jnp.dot(weighted, returned, preferred_element_type=F32)
    difference = tokens.astype(F32) + added - probe.astype(F32)
    per_token = jnp.sum(difference * difference, axis=1)
    member = (domain[:, None] == jnp.arange(domain_count, dtype=jnp.int32)[None, :]).astype(F32)
    local_loss = jnp.sum(per_token[:, None] * member, axis=0)
    loss_scale = 1.0 / math.sqrt(device_count * slot_count)
    weight_tok = jnp.sum(member * mix[None, :], axis=1)
    upstream = ((loss_scale * weight_tok)[:, None] * difference).astype(BF)
    picked_up = jnp.dot(select, upstream, preferred_element_type=F32)
    sending = (gate[:, None] * picked_up).astype(BF)
    gate_slope = jnp.sum(picked_up * returned.astype(F32), axis=1)
    logit_grad = gate_slope * gate * (1.0 - gate)
    placing = jnp.where(own_expert, logit_grad[:, None], 0.0)
    high = placing.astype(BF)
    low = (placing - high.astype(F32)).astype(BF)
    placed = lax.dot_general(
        select,
        jnp.concatenate([high, low], axis=1),
        (((0,), (0,)), ((), ())),
        preferred_element_type=F32,
    ).astype(BF)
    router_part = lax.dot_general(
        tokens, placed, (((0,), (0,)), ((), ())), preferred_element_type=F32
    )
    router_part = router_part[:, :expert_count] + router_part[:, expert_count:]
    loss_rows = jnp.zeros((8, expert_count), F32).at[0, :domain_count].set(local_loss)
    summed = lax.psum(jnp.concatenate([router_part, loss_rows], axis=0), ("dp", "expert"))
    back_grad = lax.all_to_all(
        sending.reshape(expert_count, 1, slot_count, model_width),
        "expert",
        split_axis=0,
        concat_axis=1,
        tiled=True,
    )

    def reduced(left, right):
        part = jnp.einsum("jsrd,jsrf->djf", left, right, preferred_element_type=F32)
        return lax.psum_scatter(part.astype(BF), "dp", scatter_dimension=0, tiled=True)

    grad_down = reduced(back_grad, hidden)
    hidden_grad = jnp.einsum("jsrd,djf->jsrf", back_grad, w_down, preferred_element_type=F32)
    sigmoid_gate = jax.nn.sigmoid(pre_gate)
    gate_in = (
        hidden_grad * pre_up * sigmoid_gate * (1.0 + pre_gate * (1.0 - sigmoid_gate))
    ).astype(BF)
    up_in = (hidden_grad * (pre_gate * sigmoid_gate)).astype(BF)
    grad_gate = reduced(received, gate_in)
    grad_up = reduced(received, up_in)
    domain_loss = summed[model_width, :domain_count] * (
        domain_count / (token_count * device_count * model_width)
    )
    return (domain_loss, summed[:model_width], grad_gate, grad_up, grad_down)


def solution(mesh):
    placed = (
        P(("dp", "expert"), None),
        P(("dp", "expert"), None),
        P(("dp", "expert")),
        P(),
        P(),
        P(("dp", "expert"), None, None),
        P(None, "expert", None),
        P(None, "expert", None),
        P(None, "expert", None),
    )
    return jax.shard_map(
        body,
        mesh=mesh,
        in_specs=placed,
        out_specs=(
            P(),
            P(),
            P("dp", "expert", None),
            P("dp", "expert", None),
            P("dp", "expert", None),
        ),
        check_vma=False,
    )
```

profile of v0, /device:TPU:1, one launch (start us, length us, event | category | flops | bytes accessed | tf_op | source)
XLA Modules:
  0.0 530.8 jit_solution(12913081817586084446)
XLA Ops:
  8.0 0.0 copy-start
  8.0 0.8 eq.64
  8.9 4.9 convolution_convert_fusion
  13.8 0.0 copy-start.2
  13.8 0.0 copy-start.7
  13.8 0.0 slice-start
  13.8 71.2 %all_to_all.51 = bf16[32,1,40,2048]{3,2,1,0:T(8,128)(2,1)S(1)} all-to-all(bf16[32,1,40,2048]{3,2,1,0:T(8,128)(2,1)S(1)} %bitcast.69), channel_id=1, replica_groups=mesh['dp'=8,'expert'=16] {'expert'}, dimensions={0} | all-to-all | bytes 10485760 | tf_op jit(solution)/shard_map/all_to_all | solution.py:24
  85.0 0.0 copy-done.2
  85.0 0.0 copy-start.3
  85.0 0.0 copy-done.7
  85.0 4.4 fusion.5
  89.4 0.0 copy-start.8
  89.4 0.0 copy-done.3
  89.4 0.0 slice-done
  89.4 0.0 slice-done.1
  89.4 6.5 %multiply_convert_fusion.4 = (bf16[2,16,40,768]{3,2,1,0:T(8,128)(2,1)}, f32[2,16,40,768]{3,2,1,0:T(8,128)}) fusion(f32[2,16,40,768]{3,2,1,0:T(8,128)S(1)} %fusion.5, bf16[2048,2,768,1]{2,1,0,3:T(2,128)(2,1)S(1)} %bitcast.79, bf16[16,2,1,40,2048]{4,3,1,0,2:T(8,128)(2,1)S(1)} %bitcast.71), kind=kOutput, calls=%fused_computation.31 | convolution fusion | flops 4032430080 | bytes 21364736 | tf_op jit(solution)/shard_map/jsrd,djf->jsrf/dot_general | solution.py:34
  96.0 0.0 copy-done.8
  96.0 7.7 %fusion.19 = bf16[2,16,40,2048]{3,2,1,0:T(8,128)(2,1)S(1)} fusion(bf16[2,16,40,768]{3,2,1,0:T(8,128)(2,1)} %get-tuple-element.43, bf16[2048,2,768,1]{2,1,0,3:T(2,128)(2,1)} %bitcast.80), kind=kOutput, calls=%fused_computation.28 | convolution fusion | flops 4029153280 | bytes 13500416 | tf_op jit(solution)/shard_map/jsrf,djf->jsrd/dot_general | solution.py:36
  103.6 2.8 copy.51
  106.4 5.7 %all-to-all-start.1 = ((bf16[2,16,40,2048]{3,2,0,1:T(8,128)(2,1)}), bf16[2,16,40,2048]{3,2,0,1:T(8,128)(2,1)}, u32[]{:S(2)}, u32[]{:S(2)}) async-start(bf16[2,16,40,2048]{3,2,0,1:T(8,128)(2,1)} %copy.51), calls=%async_computation.1 | async-start | bytes 10485760 | tf_op jit(solution)/shard_map/all_to_all | solution.py:37
  112.1 0.0 copy-start.4
  112.2 0.1 eq.68
  112.2 0.0 copy-done
  112.2 4.3 fusion.38
  116.6 64.9 %all-to-all-done.1 = bf16[2,16,40,2048]{3,2,0,1:T(8,128)(2,1)} async-done(((bf16[2,16,40,2048]{3,2,0,1:T(8,128)(2,1)}), bf16[2,16,40,2048]{3,2,0,1:T(8,128)(2,1)}, u32[]{:S(2)}, u32[]{:S(2)}) %all-to-all-start.1) | async-done | bytes 5242912 | tf_op jit(solution)/shard_map/all_to_all | solution.py:37
  181.5 0.0 copy-done.4
  181.5 0.0 copy-start.5
  181.5 6.5 %multiply_reduce_fusion.1 = (f32[512]{0:T(512)S(1)}, f32[512,2048]{1,0:T(8,128)S(1)}) fusion(bf16[512,2048]{1,0:T(8,128)(2,1)} %param.12, bf16[1280,2048]{1,0:T(8,128)(2,1)} %bitcast.11, s32[1280]{0:T(1024)S(1)} %eq.64, bf16[1280]{0:T(1024)(128)(2,1)S(1)} %get-tuple-element.42, bf16[512,2048]{1,0:T(8,128)(2,1)S(1)} %copy-done.4), kind=kOutput, calls=%fused_computation.25 | convolution fusion | flops 2691956224 | bytes 13641216 | tf_op jit(solution)/shard_map/dot_general | solution.py:42
  188.0 0.0 copy-done.5
  188.0 0.0 copy-done.6
  188.0 0.1 select_reduce_fusion.1
  188.1 7.4 %multiply_convert_fusion = (bf16[1280,2048]{1,0:T(8,128)(2,1)}, f32[1280]{0:T(1024)S(1)}) fusion(f32[1280]{0:T(1024)S(1)} %get-tuple-element.41, bf16[2,16,40,2048]{3,2,0,1:T(8,128)(2,1)} %all-to-all-done.1, f32[512,2048]{1,0:T(8,128)S(1)} %get-tuple-element.46, f32[512]{0:T(512)S(1)} %broadcast_multiply_fusion, s32[1280]{0:T(1024)S(1)} %eq.64), kind=kOutput, calls=%fused_computation.3 | convolution fusion | flops 2700212992 | bytes 14697472 | tf_op jit(solution)/shard_map/dot_general | solution.py:50
  195.5 14.7 %all-to-all-start.2 = ((bf16[32,1,40,2048]{3,2,1,0:T(8,128)(2,1)}), bf16[32,1,40,2048]{3,2,1,0:T(8,128)(2,1)}, u32[]{:S(2)}, u32[]{:S(2)}) async-start(bf16[32,1,40,2048]{3,2,1,0:T(8,128)(2,1)} %bitcast.74), calls=%async_computation.2 | async-start | bytes 10485760 | tf_op jit(solution)/shard_map/all_to_all | solution.py:69
  210.2 0.0 all-reduce.3.cloned.1.call-start
  210.2 0.1 copy.52
  210.4 1.0 convolution_bitcast_fusion
  211.5 0.7 select_maximum_fusion
  212.2 0.0 all-reduce.3.cloned.1.call-update
  212.2 0.0 reduce-scatter.8.cloned.1.call-start
  212.3 68.4 %all-to-all-done.2 = bf16[32,1,40,2048]{3,2,1,0:T(8,128)(2,1)} async-done(((bf16[32,1,40,2048]{3,2,1,0:T(8,128)(2,1)}), bf16[32,1,40,2048]{3,2,1,0:T(8,128)(2,1)}, u32[]{:S(2)}, u32[]{:S(2)}) %all-to-all-start.2) | async-done | bytes 5242912 | tf_op jit(solution)/shard_map/all_to_all | solution.py:69
  280.7 9.8 %fusion.2 = bf16[2048,2,768]{0,2,1:T(8,128)(2,1)} fusion(bf16[2,16,40,768]{3,2,1,0:T(8,128)(2,1)} %get-tuple-element.43, bf16[16,2,1,40,2048]{4,3,1,0,2:T(8,128)(2,1)} %bitcast.18), kind=kOutput, calls=%fused_computation.8 | convolution fusion | flops 4029677568 | bytes 13500416 | tf_op jit(solution)/shard_map/jsrd,jsrf->djf/dot_general | solution.py:78
  290.5 0.0 reduce-scatter.8.cloned.1.call-update
  290.5 0.3 reduce-scatter.6.cloned.1.call-start
  290.8 0.0 copy-start.9
  290.8 8.2 %fusion.7 = f32[2,16,40,768]{3,2,1,0:T(8,128)S(1)} fusion(bf16[2048,2,768,1]{2,1,0,3:T(2,128)(2,1)} %bitcast.81, bf16[16,2,1,40,2048]{4,3,1,0,2:T(8,128)(2,1)} %bitcast.18), kind=kOutput, calls=%fused_computation.13 | convolution fusion | flops 4026531840 | bytes 15466496 | tf_op jit(solution)/shard_map/jsrd,djf->jsrf/dot_general | solution.py:82
  299.0 0.0 copy-start.10
  299.0 1.8 copy-done.10
  300.9 0.0 copy-done.9
  300.9 9.9 %fusion.1 = bf16[2048,2,768]{0,2,1:T(8,128)(2,1)} fusion(bf16[16,2,1,40,2048]{4,3,1,0,2:T(8,128)(2,1)} %bitcast.72, f32[2,16,40,768]{3,2,1,0:T(8,128)S(1)} %fusion.7, f32[2,16,40,768]{3,2,1,0:T(8,128)S(1)} %copy-done.9), kind=kOutput, calls=%fused_computation.7 | convolution fusion | flops 4035575808 | bytes 19398656 | tf_op jit(solution)/shard_map/jsrd,jsrf->djf/dot_general | solution.py:78
  310.8 0.0 reduce-scatter.6.cloned.1.call-update
  310.8 0.0 reduce-scatter.4.cloned.1.call-start
  310.8 12.3 %fusion = bf16[2048,2,768]{0,2,1:T(8,128)(2,1)} fusion(bf16[16,2,1,40,2048]{4,3,1,0,2:T(8,128)(2,1)} %bitcast.73, f32[2,16,40,768]{3,2,1,0:T(8,128)} %copy-done.8, f32[2,16,40,768]{3,2,1,0:T(8,128)} %copy-done.10, f32[2,16,40,768]{3,2,1,0:T(8,128)} %get-tuple-element.44), kind=kOutput, calls=%fused_computation.6 | convolution fusion | flops 4039507968 | bytes 23330816 | tf_op jit(solution)/shard_map/jsrd,jsrf->djf/dot_general | solution.py:78
  323.1 0.0 reduce-scatter.4.cloned.1.call-update
  323.1 0.0 copy-start.1
  323.2 129.6 %all-reduce.3.cloned.1.call-done = f32[2056,32]{0,1:T(8,128)} async-done(((f32[2056,32]{0,1:T(8,128)}), f32[2056,32]{0,1:T(8,128)}) %all-reduce.3.cloned.1.call-update) | async-done | bytes 263184 | tf_op jit(solution)/shard_map/psum | solution.py:68
  452.8 1.7 slice.35
  454.4 1.3 fusion.49
  455.8 0.0 reduce-scatter.8.cloned.1.call-done
  455.8 3.1 copy.58
  458.9 0.0 reduce-scatter.6.cloned.1.call-done
  458.9 3.0 copy.57
  461.9 58.3 %reduce-scatter.4.cloned.1.call-done = bf16[256,2,768]{0,2,1:T(8,128)(2,1)} async-done(((bf16[2048,2,768]{0,2,1:T(8,128)(2,1)}), bf16[256,2,768]{0,2,1:T(8,128)(2,1)}) %reduce-scatter.4.cloned.1.call-update) | async-done | bytes 786448 | tf_op jit(solution)/shard_map/reduce_scatter | solution.py:79
  520.2 3.0 copy.56
  523.3 0.0 copy-done.1
  (10 shorter events, 0.1 us)
Async XLA Ops:
  8.0 104.2 %copy-start = (bf16[2048,32]{0,1:T(8,128)(2,1)S(1)}, bf16[2048,32]{0,1:T(8,128)(2,1)}, u32[]{:S(2)}) copy-start(bf16[2048,32]{0,1:T(8,128)(2,1)} %param.15) | copy-start | bytes 393220
  13.8 71.2 %copy-start.2 = (bf16[1280,2048]{1,0:T(8,128)(2,1)}, bf16[1280,2048]{1,0:T(8,128)(2,1)S(1)}, u32[]{:S(2)}) copy-start(bf16[1280,2048]{1,0:T(8,128)(2,1)S(1)} %convolution_convert_fusion) | copy-start | bytes 15728644
  13.8 71.2 %copy-start.7 = (bf16[2048,2,768]{2,1,0:T(2,128)(2,1)S(1)}, bf16[2048,2,768]{2,1,0:T(2,128)(2,1)}, u32[]{:S(2)}) copy-start(bf16[2048,2,768]{2,1,0:T(2,128)(2,1)} %param.17) | copy-start | bytes 18874372
  13.8 75.6 %slice-start = ((s8[6291456]{0:T(1024)(128)(4,1)}), s8[4194304]{0:T(1024)(128)(4,1)S(1)}, s32[]{:S(2)}) async-start(s8[6291456]{0:T(1024)(128)(4,1)} %bitcast.77), calls=%async_computation.10 | async-start | bytes 8388608
  85.0 4.4 copy-start.3
  85.0 4.4 slice-start.1
  89.4 6.6 %copy-start.8 = (f32[2,16,40,768]{3,2,1,0:T(8,128)}, f32[2,16,40,768]{3,2,1,0:T(8,128)S(1)}, u32[]{:S(2)}) copy-start(f32[2,16,40,768]{3,2,1,0:T(8,128)S(1)} %fusion.5) | copy-start | bytes 11796484
  106.4 75.0 %all-to-all-start.1 = ((bf16[2,16,40,2048]{3,2,0,1:T(8,128)(2,1)}), bf16[2,16,40,2048]{3,2,0,1:T(8,128)(2,1)}, u32[]{:S(2)}, u32[]{:S(2)}) async-start(bf16[2,16,40,2048]{3,2,0,1:T(8,128)(2,1)} %copy.51), calls=%async_computation.1 | async-start | bytes 10485760 | tf_op jit(solution)/shard_map/all_to_all | solution.py:37
  112.1 69.3 %copy-start.4 = (bf16[512,2048]{1,0:T(8,128)(2,1)S(1)}, bf16[512,2048]{1,0:T(8,128)(2,1)}, u32[]{:S(2)}) copy-start(bf16[512,2048]{1,0:T(8,128)(2,1)} %param.11) | copy-start | bytes 6291460
  181.5 6.5 %copy-start.5 = (s32[512]{0:T(512)S(1)}, s32[512]{0:T(512)}, u32[]{:S(2)}) copy-start(s32[512]{0:T(512)} %param.13) | copy-start | bytes 6148
  181.5 6.5 %copy-start.6 = (f32[22]{0:T(128)S(1)}, f32[22]{0:T(128)}, u32[]{:S(2)}) copy-start(f32[22]{0:T(128)} %param.14) | copy-start | bytes 268
  195.5 85.2 %all-to-all-start.2 = ((bf16[32,1,40,2048]{3,2,1,0:T(8,128)(2,1)}), bf16[32,1,40,2048]{3,2,1,0:T(8,128)(2,1)}, u32[]{:S(2)}, u32[]{:S(2)}) async-start(bf16[32,1,40,2048]{3,2,1,0:T(8,128)(2,1)} %bitcast.74), calls=%async_computation.2 | async-start | bytes 10485760 | tf_op jit(solution)/shard_map/all_to_all | solution.py:69
  210.2 242.6 %all-reduce.3.cloned.1.call-start = ((), (), s32[]{:S(2)}) async-start(), calls=%async_computation.6 | async-start | bytes 557056 | tf_op jit(solution)/shard_map/psum | solution.py:68
  212.2 243.5 %reduce-scatter.8.cloned.1.call-start = ((), (), s32[]{:S(2)}) async-start(), calls=%async_computation.9 | async-start | bytes 7077888 | tf_op jit(solution)/shard_map/reduce_scatter | solution.py:79
  290.5 168.3 %reduce-scatter.6.cloned.1.call-start = ((), (), s32[]{:S(2)}) async-start(), calls=%async_computation.8 | async-start | bytes 7077888 | tf_op jit(solution)/shard_map/reduce_scatter | solution.py:79
  290.8 10.1 %copy-start.9 = (f32[2,16,40,768]{3,2,1,0:T(8,128)S(1)}, f32[2,16,40,768]{3,2,1,0:T(8,128)}, u32[]{:S(2)}) copy-start(f32[2,16,40,768]{3,2,1,0:T(8,128)} %copy-done.8) | copy-start | bytes 11796484
  299.0 1.9 copy-start.10
  310.8 209.4 %reduce-scatter.4.cloned.1.call-start = ((), (), s32[]{:S(2)}) async-start(), calls=%async_computation.7 | async-start | bytes 7077888 | tf_op jit(solution)/shard_map/reduce_scatter | solution.py:79
  323.1 200.1 %copy-start.1 = (bf16[2048,32]{0,1:T(8,128)(2,1)S(1)}, bf16[2048,32]{0,1:T(8,128)(2,1)}, u32[]{:S(2)}) copy-start(bf16[2048,32]{0,1:T(8,128)(2,1)} %param.15) | copy-start | bytes 393220
Sparse Core Ops, SparseCore 0:
  216.3 236.3 all-reduce.2
Sparse Core Ops, SparseCore 1:
  290.6 81.2 reduce-scatter.7
  374.2 71.8 reduce-scatter.5
  448.3 71.9 reduce-scatter.3
where the time goes:
time: 531 us
  waiting for transfers between devices  321 us (60%)
  matrix products  82.8 us (16%)
  blocking collectives  71.2 us (13%)
  starting transfers between devices  20.8 us (4%)
  local copies, waits for them, and re-layouts  16.6 us (3%)
  between operations  15.9 us (3%)
    psum x1, waiting for transfers between devices, body(): lax.psum(jnp.concatenate([router_part, loss_rows], axis=0), ('dp', 'exper...  130 us
    all_to_all x1, blocking collectives, body(): lax.all_to_all(outgoing.reshape(expert_count, 1, slot_count, model_width)...  71.2 us
    all_to_all x1, waiting for transfers between devices, body(): lax.all_to_all(sending.reshape(expert_count, 1, slot_count, model_width),...  68.4 us
    all_to_all x1, waiting for transfers between devices, body(): lax.all_to_all(result, 'expert', split_axis=1, concat_axis=0, tiled=True)  64.9 us
    reduce_scatter x3, waiting for transfers between devices, reduced(): lax.psum_scatter(part.astype(BF), 'dp', scatter_dimension=0, tiled=True)  58.3 us
    dot_general x3, matrix products, reduced(): part = jnp.einsum('jsrd,jsrf->djf', left, right, preferred_element_type=F32)  32 us
    all_to_all x1, starting transfers between devices, body(): lax.all_to_all(sending.reshape(expert_count, 1, slot_count, model_width),...  14.7 us
    unnamed x29, local copies, waits for them, and re-layouts  11.1 us
  transfers between devices with their start and end apart: 6, of which 4 were waited for; matrix products, arithmetic and copies ran while one was open for 10% of the time, Pallas kernels for 0%

commit v1 on v0

--- a/solution.py
+++ b/solution.py
@@ -65,7 +65,9 @@
     )
     router_part = router_part[:, :expert_count] + router_part[:, expert_count:]
     loss_rows = jnp.zeros((8, expert_count), F32).at[0, :domain_count].set(local_loss)
-    summed = lax.psum(jnp.concatenate([router_part, loss_rows], axis=0), ("dp", "expert"))
+    summed = jax.lax.all_gather(
+        jnp.concatenate([router_part, loss_rows], axis=0), ("dp", "expert")
+    ).sum(axis=0)
     back_grad = lax.all_to_all(
         sending.reshape(expert_count, 1, slot_count, model_width),
         "expert",

time: 531 us -> 705 us (1.33)
  waiting for transfers between devices: 321 us -> 425 us
  blocking collectives: 71.2 us -> 148 us
  starting transfers between devices: 20.8 us -> 6.05 us
  other arithmetic: 2.29 us -> 13.7 us
    reduce_scatter x3, waiting for transfers between devices: 58.3 us -> 232 us  [reduced(): lax.psum_scatter(part.astype(BF), 'dp', scatter_dimension=0, tiled=True)]
    psum x1 -> x0, waiting for transfers between devices: 130 us -> none  [body(): lax.psum(jnp.concatenate([router_part, loss_rows], axis=0), ('dp', 'exper...]
    all_gather x0 -> x1, waiting for transfers between devices: none -> 128 us  [body(): jax.lax.all_gather(jnp.concatenate([router_part, loss_rows], axis=0), ('d...]
    all_to_all x0 -> x1, blocking collectives: none -> 76.5 us  [body(): lax.all_to_all(sending.reshape(expert_count, 1, slot_count, model_width),...]
    all_to_all x1 -> x0, waiting for transfers between devices: 68.4 us -> none  [body(): lax.all_to_all(sending.reshape(expert_count, 1, slot_count, model_width),...]
    all_to_all x1 -> x0, starting transfers between devices: 14.7 us -> none  [body(): lax.all_to_all(sending.reshape(expert_count, 1, slot_count, model_width),...]
    reduce_sum x0 -> x1, other arithmetic: none -> 12.1 us  [body(): summed = jax.lax.all_gather(jnp.concatenate([router_part, loss_rows], axi...]
  transfers between devices with their start and end apart: 6 -> 5, of which waited for: 4 -> 5; matrix products, arithmetic and copies ran while one was open for 10% -> 7% of each run, Pallas kernels for 0% -> 0%
where the time goes in v1:
time: 705 us
  waiting for transfers between devices  425 us (60%)
  blocking collectives  148 us (21%)
  matrix products  78.8 us (11%)
  local copies, waits for them, and re-layouts  17.9 us (3%)
  between operations  15.4 us (2%)
  other arithmetic  13.7 us (2%)
    reduce_scatter x3, waiting for transfers between devices, reduced(): lax.psum_scatter(part.astype(BF), 'dp', scatter_dimension=0, tiled=True)  232 us
    all_gather x1, waiting for transfers between devices, body(): jax.lax.all_gather(jnp.concatenate([router_part, loss_rows], axis=0), ('d...  128 us
    all_to_all x1, blocking collectives, body(): lax.all_to_all(sending.reshape(expert_count, 1, slot_count, model_width),...  76.5 us
    all_to_all x1, blocking collectives, body(): lax.all_to_all(outgoing.reshape(expert_count, 1, slot_count, model_width)...  71.2 us
    all_to_all x1, waiting for transfers between devices, body(): lax.all_to_all(result, 'expert', split_axis=1, concat_axis=0, tiled=True)  64.9 us
    dot_general x3, matrix products, reduced(): part = jnp.einsum('jsrd,jsrf->djf', left, right, preferred_element_type=F32)  29.4 us
  transfers between devices with their start and end apart: 5, of which 5 were waited for; matrix products, arithmetic and copies ran while one was open for 7% of the time, Pallas kernels for 0%

profile of v1, /device:TPU:1, one launch (start us, length us, event | category | flops | bytes accessed | tf_op | source)
XLA Modules:
  0.0 704.9 jit_solution(6079947111055324759)
XLA Ops:
  8.0 0.0 copy-start
  8.0 0.8 eq.64
  8.9 4.9 convolution_convert_fusion
  13.8 0.0 copy-start.2
  13.8 0.0 copy-start.8
  13.8 0.0 slice-start
  13.8 71.2 %all_to_all.51 = bf16[32,1,40,2048]{3,2,1,0:T(8,128)(2,1)S(1)} all-to-all(bf16[32,1,40,2048]{3,2,1,0:T(8,128)(2,1)S(1)} %bitcast.71), channel_id=1, replica_groups=mesh['dp'=8,'expert'=16] {'expert'}, dimensions={0} | all-to-all | bytes 10485760 | tf_op jit(solution)/shard_map/all_to_all | solution.py:24
  85.0 0.0 copy-done.2
  85.0 0.0 copy-start.3
  85.0 0.0 copy-done.8
  85.0 4.4 fusion.5
  89.4 0.0 copy-start.9
  89.4 0.0 copy-done.3
  89.4 0.0 slice-done
  89.4 0.0 slice-done.1
  89.4 6.5 multiply_convert_fusion.4
  96.0 0.0 copy-done.9
  96.0 7.7 %fusion.19 = bf16[2,16,40,2048]{3,2,1,0:T(8,128)(2,1)S(1)} fusion(bf16[2,16,40,768]{3,2,1,0:T(8,128)(2,1)} %get-tuple-element.43, bf16[2048,2,768,1]{2,1,0,3:T(2,128)(2,1)} %bitcast.84), kind=kOutput, calls=%fused_computation.28 | convolution fusion | flops 4029153280 | bytes 13500416 | tf_op jit(solution)/shard_map/jsrf,djf->jsrd/dot_general | solution.py:36
  103.7 2.7 copy.51
  106.4 5.7 all-to-all-start.1
  112.0 0.0 reduce-scatter.8.cloned.1.call-start
  112.1 0.1 eq.68
  112.2 0.0 copy-done
  112.2 4.3 fusion.38
  116.5 64.9 %all-to-all-done.1 = bf16[2,16,40,2048]{3,2,0,1:T(8,128)(2,1)} async-done(((bf16[2,16,40,2048]{3,2,0,1:T(8,128)(2,1)}), bf16[2,16,40,2048]{3,2,0,1:T(8,128)(2,1)}, u32[]{:S(2)}, u32[]{:S(2)}) %all-to-all-start.1) | async-done | bytes 5242912 | tf_op jit(solution)/shard_map/all_to_all | solution.py:37
  181.4 0.0 copy-done.5
  181.4 6.5 multiply_reduce_fusion.1
  187.9 0.0 copy-done.6
  187.9 0.0 copy-done.7
  187.9 0.1 select_reduce_fusion.1
  188.0 5.9 multiply_convert_fusion
  194.0 0.0 copy-start.12
  194.0 76.5 %all_to_all.52 = bf16[32,1,40,2048]{3,2,1,0:T(8,128)(2,1)S(1)} all-to-all(bf16[32,1,40,2048]{3,2,1,0:T(8,128)(2,1)S(1)} %bitcast.78), channel_id=1, replica_groups=mesh['dp'=8,'expert'=16] {'expert'}, dimensions={0} | all-to-all | bytes 10485760 | tf_op jit(solution)/shard_map/all_to_all | solution.py:71
  270.4 2.3 copy-done.4
  272.8 0.0 copy-done.12
  272.8 7.1 %fusion.2 = bf16[2048,2,768]{0,2,1:T(8,128)(2,1)} fusion(bf16[2,16,40,768]{3,2,1,0:T(8,128)(2,1)S(1)} %copy-done.12, bf16[16,2,1,40,2048]{4,3,1,0,2:T(8,128)(2,1)S(1)} %bitcast.76), kind=kOutput, calls=%fused_computation.8 | convolution fusion | flops 4029677568 | bytes 13500416 | tf_op jit(solution)/shard_map/jsrd,jsrf->djf/dot_general | solution.py:80
  279.9 0.0 reduce-scatter.8.cloned.1.call-update
  279.9 0.3 reduce-scatter.6.cloned.1.call-start
  280.2 0.0 copy-start.10
  280.2 8.2 %fusion.7 = f32[2,16,40,768]{3,2,1,0:T(8,128)S(1)} fusion(bf16[2048,2,768,1]{2,1,0,3:T(2,128)(2,1)} %bitcast.85, bf16[16,2,1,40,2048]{4,3,1,0,2:T(8,128)(2,1)} %bitcast.77), kind=kOutput, calls=%fused_computation.13 | convolution fusion | flops 4026531840 | bytes 15466496 | tf_op jit(solution)/shard_map/jsrd,djf->jsrf/dot_general | solution.py:84
  288.4 0.0 copy-start.11
  288.4 1.9 copy-done.11
  290.3 0.0 copy-done.10
  290.3 9.9 %fusion.1 = bf16[2048,2,768]{0,2,1:T(8,128)(2,1)} fusion(bf16[16,2,1,40,2048]{4,3,1,0,2:T(8,128)(2,1)} %bitcast.74, f32[2,16,40,768]{3,2,1,0:T(8,128)S(1)} %fusion.7, f32[2,16,40,768]{3,2,1,0:T(8,128)S(1)} %copy-done.10), kind=kOutput, calls=%fused_computation.7 | convolution fusion | flops 4035575808 | bytes 19398656 | tf_op jit(solution)/shard_map/jsrd,jsrf->djf/dot_general | solution.py:80
  300.2 0.0 reduce-scatter.6.cloned.1.call-update
  300.2 0.0 reduce-scatter.4.cloned.1.call-start
  300.2 12.4 %fusion = bf16[2048,2,768]{0,2,1:T(8,128)(2,1)} fusion(bf16[16,2,1,40,2048]{4,3,1,0,2:T(8,128)(2,1)} %bitcast.75, f32[2,16,40,768]{3,2,1,0:T(8,128)} %copy-done.9, f32[2,16,40,768]{3,2,1,0:T(8,128)} %copy-done.11, f32[2,16,40,768]{3,2,1,0:T(8,128)} %get-tuple-element.44), kind=kOutput, calls=%fused_computation.6 | convolution fusion | flops 4039507968 | bytes 23330816 | tf_op jit(solution)/shard_map/jsrd,jsrf->djf/dot_general | solution.py:80
  312.7 0.0 reduce-scatter.4.cloned.1.call-update
  312.7 0.0 all-gather.4.cloned.1.call-start
  312.7 0.1 copy.52
  312.9 1.0 convolution_bitcast_fusion
  314.0 0.7 fusion.42
  314.7 0.0 all-gather.4.cloned.1.call-update
  314.8 45.7 %reduce-scatter.8.cloned.1.call-done = bf16[256,2,768]{0,2,1:T(8,128)(2,1)} async-done(((bf16[2048,2,768]{0,2,1:T(8,128)(2,1)}), bf16[256,2,768]{0,2,1:T(8,128)(2,1)}) %reduce-scatter.8.cloned.1.call-update) | async-done | bytes 786448 | tf_op jit(solution)/shard_map/reduce_scatter | solution.py:81
  360.5 3.1 copy.58
  363.5 93.2 %reduce-scatter.6.cloned.1.call-done = bf16[256,2,768]{0,2,1:T(8,128)(2,1)} async-done(((bf16[2048,2,768]{0,2,1:T(8,128)(2,1)}), bf16[256,2,768]{0,2,1:T(8,128)(2,1)}) %reduce-scatter.6.cloned.1.call-update) | async-done | bytes 786448 | tf_op jit(solution)/shard_map/reduce_scatter | solution.py:81
  456.7 3.1 copy.57
  459.7 93.4 %reduce-scatter.4.cloned.1.call-done = bf16[256,2,768]{0,2,1:T(8,128)(2,1)} async-done(((bf16[2048,2,768]{0,2,1:T(8,128)(2,1)}), bf16[256,2,768]{0,2,1:T(8,128)(2,1)}) %reduce-scatter.4.cloned.1.call-update) | async-done | bytes 786448 | tf_op jit(solution)/shard_map/reduce_scatter | solution.py:81
  553.2 3.0 copy.56
  556.2 128.1 %all-gather.4.cloned.1.call-done = f32[128,2056,32]{1,2,0:T(8,128)} async-done(((f32[1,2056,32]{1,2,0:T(8,128)}), f32[128,2056,32]{1,2,0:T(8,128)}) %all-gather.4.cloned.1.call-update) | async-done | bytes 33685520 | tf_op jit(solution)/shard_map/all_gather | solution.py:68
  684.3 12.1 %reduce_sum.59 = f32[2056,32]{0,1:T(8,128)S(1)} reduce(f32[128,2056,32]{1,2,0:T(8,128)} %all-gather.4.cloned.1.call-done, f32[]{:T(128)} %constant.36.clone.1), dimensions={0}, to_apply=%region_5.6 | reduce | flops 8355584 | bytes 33948676 | tf_op jit(solution)/shard_map/reduce_sum | solution.py:70
  696.4 0.7 slice.35
  697.1 0.6 fusion.50
  697.8 0.0 copy-done.1
  (14 shorter events, 0.1 us)
Async XLA Ops:
  8.0 104.2 %copy-start = (bf16[2048,32]{0,1:T(8,128)(2,1)S(1)}, bf16[2048,32]{0,1:T(8,128)(2,1)}, u32[]{:S(2)}) copy-start(bf16[2048,32]{0,1:T(8,128)(2,1)} %param.15) | copy-start | bytes 393220
  13.8 71.2 %copy-start.2 = (bf16[1280,2048]{1,0:T(8,128)(2,1)}, bf16[1280,2048]{1,0:T(8,128)(2,1)S(1)}, u32[]{:S(2)}) copy-start(bf16[1280,2048]{1,0:T(8,128)(2,1)S(1)} %convolution_convert_fusion) | copy-start | bytes 15728644
  13.8 71.2 %copy-start.8 = (bf16[2048,2,768]{2,1,0:T(2,128)(2,1)S(1)}, bf16[2048,2,768]{2,1,0:T(2,128)(2,1)}, u32[]{:S(2)}) copy-start(bf16[2048,2,768]{2,1,0:T(2,128)(2,1)} %param.17) | copy-start | bytes 18874372
  13.8 75.6 %slice-start = ((s8[6291456]{0:T(1024)(128)(4,1)}), s8[4194304]{0:T(1024)(128)(4,1)S(1)}, s32[]{:S(2)}) async-start(s8[6291456]{0:T(1024)(128)(4,1)} %bitcast.81), calls=%async_computation.10 | async-start | bytes 8388608
  85.0 4.4 copy-start.3
  85.0 4.4 slice-start.1
  89.4 6.6 copy-start.9
  106.4 75.0 %all-to-all-start.1 = ((bf16[2,16,40,2048]{3,2,0,1:T(8,128)(2,1)}), bf16[2,16,40,2048]{3,2,0,1:T(8,128)(2,1)}, u32[]{:S(2)}, u32[]{:S(2)}) async-start(bf16[2,16,40,2048]{3,2,0,1:T(8,128)(2,1)} %copy.51), calls=%async_computation.1 | async-start | bytes 10485760 | tf_op jit(solution)/shard_map/all_to_all | solution.py:37
  112.0 69.3 %copy-start.5 = (bf16[512,2048]{1,0:T(8,128)(2,1)S(1)}, bf16[512,2048]{1,0:T(8,128)(2,1)}, u32[]{:S(2)}) copy-start(bf16[512,2048]{1,0:T(8,128)(2,1)} %param.11) | copy-start | bytes 6291460
  112.0 248.4 %reduce-scatter.8.cloned.1.call-start = ((), (), s32[]{:S(2)}) async-start(), calls=%async_computation.8 | async-start | bytes 7077888 | tf_op jit(solution)/shard_map/reduce_scatter | solution.py:81
  181.4 6.5 copy-start.6
  181.4 6.5 copy-start.7
  194.0 78.8 %copy-start.12 = (bf16[2,16,40,768]{3,2,1,0:T(8,128)(2,1)S(1)}, bf16[2,16,40,768]{3,2,1,0:T(8,128)(2,1)}, u32[]{:S(2)}) copy-start(bf16[2,16,40,768]{3,2,1,0:T(8,128)(2,1)} %get-tuple-element.43) | copy-start | bytes 5898244
  270.4 2.3 copy-start.4
  279.9 176.8 %reduce-scatter.6.cloned.1.call-start = ((), (), s32[]{:S(2)}) async-start(), calls=%async_computation.7 | async-start | bytes 7077888 | tf_op jit(solution)/shard_map/reduce_scatter | solution.py:81
  280.2 10.1 %copy-start.10 = (f32[2,16,40,768]{3,2,1,0:T(8,128)S(1)}, f32[2,16,40,768]{3,2,1,0:T(8,128)}, u32[]{:S(2)}) copy-start(f32[2,16,40,768]{3,2,1,0:T(8,128)} %copy-done.9) | copy-start | bytes 11796484
  288.4 1.9 copy-start.11
  300.2 253.0 %reduce-scatter.4.cloned.1.call-start = ((), (), s32[]{:S(2)}) async-start(), calls=%async_computation.6 | async-start | bytes 7077888 | tf_op jit(solution)/shard_map/reduce_scatter | solution.py:81
  312.7 371.6 %all-gather.4.cloned.1.call-start = ((), (), s32[]{:S(2)}) async-start(), calls=%async_computation.9 | async-start | bytes 35930112 | tf_op jit(solution)/shard_map/all_gather | solution.py:68
  684.3 13.5 %copy-start.1 = (bf16[2048,32]{0,1:T(8,128)(2,1)S(1)}, bf16[2048,32]{0,1:T(8,128)(2,1)}, u32[]{:S(2)}) copy-start(bf16[2048,32]{0,1:T(8,128)(2,1)} %param.15) | copy-start | bytes 393220
Sparse Core Ops, SparseCore 0:
  280.0 80.4 reduce-scatter.7
  362.9 93.7 reduce-scatter.5
  459.1 94.0 reduce-scatter.3
Sparse Core Ops, SparseCore 1:
  314.9 369.3 all-gather.3
